TPU v7x, 256 devices: a whole 4x4x8 slice. The times are simulated.
256 devices in a mesh: enc: 16 (over z, core), vocab: 8 (over x, y_hi), grp: 2 (over y_lo).
Axes of the slice: x: 4, y: 4 (y_hi: 2, y_lo: 2; y = y_hi * 2 + y_lo), z: 8, core: 2. Of those that a mesh axis runs over, the one named last changes fastest.
Arguments:
- hidden: bfloat16 [12288, 1024], P('enc', ('vocab', 'grp')), may hold values from -6 to 6
- dense_weight: bfloat16 [1024, 1024], P('enc'), may hold values from -0.1875 to 0.1875
- head_weight: bfloat16 [1024, 126976], P('enc', ('vocab', 'grp')), may hold values from -0.1875 to 0.1875
- head_bias: float32 [126976], P(('vocab', 'grp')), may hold values from -4 to 4
- lengths: int32 [48], P('enc'), may hold values from 64 to 256, as said below
- queries: bfloat16 [128, 126976], P('enc', ('vocab', 'grp')), may hold values from -0.25 to 0.25283518
- positives: int32 [128], replicated, may hold values from 0 to 47
Outputs:
- batch_loss: float32 [], replicated
- query_grad: float32 [128, 126976], P('enc', ('vocab', 'grp'))
- passage_grad: float32 [48, 126976], P('enc', ('vocab', 'grp'))
Inputs may be any that keep to these rules, and one draw needn't show every extreme that they name: `lengths`: each 3 passages in a row hold, among their first two, one with 256 valid tokens and one with 64.
All inputs are finite; a program needn't handle non-finite values.
Results may differ from a plain program's by a relative error of at most 0.035.
Values may be sent and summed in bfloat16 or wider, within the bound.
A program may use at most 128 MiB of HBM per device.

v0:
```python
import jax
import jax.numpy as jnp
from jax import lax
from jax.sharding import PartitionSpec as P


def finish_norm(pre_act):
    activated = jax.nn.gelu(pre_act, approximate=False)
    center = jnp.mean(activated, axis=-1, keepdims=True)
    spread = jnp.mean(jnp.square(activated - center), axis=-1, keepdims=True)
    return ((activated - center) * lax.rsqrt(spread + 1e-05)).astype(jnp.bfloat16)


def project(in_rows, dense_weight):
    pre_act = jnp.dot(
        in_rows,
        lax.all_gather(dense_weight, "enc", axis=0, tiled=True),
        preferred_element_type=jnp.float32,
    )
    return finish_norm(pre_act)


def pool_reps(logits, token_counts, seq_len):
    passages = token_counts.shape[0]
    by_passage = logits.reshape(passages, seq_len, logits.shape[1])
    positions = lax.broadcasted_iota(jnp.int32, (passages, seq_len), 1)
    is_valid = positions < token_counts[:, None]
    masked = jnp.where(is_valid[:, :, None], by_passage, -jnp.inf)
    peak_val = jnp.max(masked, axis=1)
    return jnp.log1p(jnp.maximum(peak_val, 0.0)).astype(jnp.bfloat16)


def softmax_grads(scores, chosen):
    peak_val = jnp.max(scores, axis=1, keepdims=True)
    log_total = jnp.log(jnp.sum(jnp.exp(scores - peak_val), axis=1, keepdims=True)) + peak_val
    columns = lax.broadcasted_iota(jnp.int32, scores.shape, 1)
    is_positive = columns == chosen[:, None]
    picked_score = jnp.sum(jnp.where(is_positive, scores, 0.0), axis=1)
    batch_loss = jnp.sum(log_total[:, 0] - picked_score)
    score_grad = (jnp.exp(scores - log_total) - is_positive.astype(jnp.float32)).astype(
        jnp.bfloat16
    )
    return (batch_loss, score_grad)


def per_device(hidden, dense_weight, head_weight, head_bias, lengths, queries, positives):
    pass_dev = lengths.shape[0]
    seq_len = hidden.shape[0] // pass_dev
    enc_index = lax.axis_index("enc")
    features_all = lax.all_gather(hidden, ("vocab", "grp"), axis=1, tiled=True)
    normed = project(features_all, dense_weight)
    logits = jnp.dot(
        normed,
        lax.all_gather(head_weight, "enc", axis=0, tiled=True),
        preferred_element_type=jnp.float32,
    )
    pass_reps = pool_reps(logits + head_bias, lengths, seq_len)
    all_queries = lax.all_gather(queries, "enc", axis=0, tiled=True)
    partial_value = lax.dot_general(
        all_queries, pass_reps, (((1,), (1,)), ((), ())), preferred_element_type=jnp.float32
    )
    local_scores = lax.psum(partial_value, ("vocab", "grp"))
    scores = lax.all_gather(local_scores, "enc", axis=1, tiled=True)
    loss_sum, score_grad = softmax_grads(scores, positives)
    batch_loss = loss_sum / scores.shape[0]
    own_grad = lax.dynamic_slice_in_dim(score_grad, enc_index * pass_dev, pass_dev, 1)
    query_grad = lax.psum_scatter(
        jnp.dot(own_grad, pass_reps, preferred_element_type=jnp.float32),
        "enc",
        scatter_dimension=0,
        tiled=True,
    )
    passage_grad = lax.dot_general(
        own_grad, all_queries, (((0,), (0,)), ((), ())), preferred_element_type=jnp.float32
    )
    return (batch_loss, query_grad, passage_grad)


def solution(mesh):
    placed = (
        P("enc", ("vocab", "grp")),
        P("enc", None),
        P("enc", ("vocab", "grp")),
        P(("vocab", "grp")),
        P("enc"),
        P("enc", ("vocab", "grp")),
        P(),
    )
    return jax.shard_map(
        per_device,
        mesh=mesh,
        in_specs=placed,
        out_specs=(P(), P("enc", ("vocab", "grp")), P("enc", ("vocab", "grp"))),
        check_vma=False,
    )
```

profile of v0, /device:TPU:2, one launch (start us, length us, event | category | flops | bytes accessed | tf_op | source)
XLA Modules:
  0.0 363.2 jit_solution(3995243074012879067)
XLA Ops:
  7.2 0.0 all-gather.6.cloned.1.call-start
  7.2 0.7 all-gather.6.cloned.1.call-update
  7.9 0.0 all-gather.8.cloned.1.call-start
  7.9 0.7 all-gather.8.cloned.1.call-update
  8.6 0.0 all-gather.10.cloned.1.call-start
  8.7 0.7 all-gather.10.cloned.1.call-update
  9.4 0.0 all-gather.12.cloned.1.call-start
  9.4 0.5 all-gather.12.cloned.1.call-update
  10.0 0.0 reduce-scatter.2.cloned.1.call-start
  10.0 0.7 iota_compare_fusion.1
  10.7 0.7 iota_compare_fusion
  11.4 50.6 %all-gather.6.cloned.1.call-done = bf16[768,1024]{0,1:T(8,128)(2,1)} async-done(((bf16[768,64]{0,1:T(8,128)(2,1)}), bf16[768,1024]{0,1:T(8,128)(2,1)}) %all-gather.6.cloned.1.call-update) | async-done | bytes 1572880 | tf_op jit(solution)/shard_map/all_gather | solution.py:50
  62.0 41.4 %all-gather.8.cloned.1.call-done = bf16[1024,1024]{1,0:T(8,128)(2,1)} async-done(((bf16[64,1024]{1,0:T(8,128)(2,1)}), bf16[1024,1024]{1,0:T(8,128)(2,1)}) %all-gather.8.cloned.1.call-update) | async-done | bytes 2097168 | tf_op jit(solution)/shard_map/all_gather | solution.py:17
  103.4 10.5 %fusion.17 = (f32[768]{0:T(1024)S(1)}, f32[768,1024]{1,0:T(8,128)S(1)}) fusion(bf16[768,1024]{0,1:T(8,128)(2,1)} %all-gather.6.cloned.1.call-done, bf16[1024,1024]{1,0:T(8,128)(2,1)} %all-gather.8.cloned.1.call-done), kind=kOutput, calls=%fused_computation.41 | convolution fusion | flops 1661730048 | bytes 6818816 | tf_op jit(solution)/shard_map/dot_general | solution.py:15
  114.0 0.0 copy-start.2
  114.0 0.4 multiply_reduce_fusion
  114.5 82.1 %all-gather.10.cloned.1.call-done = bf16[1024,7936]{1,0:T(8,128)(2,1)} async-done(((bf16[64,7936]{1,0:T(8,128)(2,1)}), bf16[1024,7936]{1,0:T(8,128)(2,1)}) %all-gather.10.cloned.1.call-update) | async-done | bytes 16252944 | tf_op jit(solution)/shard_map/all_gather | solution.py:54
  196.5 0.0 copy-done.2
  196.5 21.4 %convolution_add_fusion = f32[768,7936]{1,0:T(8,128)} fusion(bf16[1024,7936]{1,0:T(8,128)(2,1)} %all-gather.10.cloned.1.call-done, f32[7936]{0:T(1024)S(1)} %copy-done.2, f32[768,1024]{1,0:T(8,128)S(1)} %get-tuple-element.8, f32[768]{0:T(1024)S(1)} %add_rsqrt_fusion, f32[768]{0:T(1024)S(1)} %broadcast_multiply_fusion), kind=kOutput, calls=%fused_computation.1 | convolution fusion | flops 12490702848 | bytes 43815936 | tf_op jit(solution)/shard_map/dot_general | solution.py:52
  217.9 0.0 copy-start.1
  217.9 9.4 %select_reduce_fusion = f32[3,7936]{1,0:T(4,128)S(1)} fusion(f32[3,256,7936]{2,1,0:T(8,128)} %bitcast.14, pred[3,256]{1,0:T(4,128)(4,1)S(1)} %iota_compare_fusion.1), kind=kLoop, calls=%fused_computation | loop fusion | flops 12165888 | bytes 24475392 | tf_op jit(solution)/shard_map/reduce_max | solution.py:29
  227.4 9.2 %all-gather.12.cloned.1.call-done = bf16[128,7936]{1,0:T(8,128)(2,1)} async-done(((bf16[8,7936]{1,0:T(8,128)(2,1)}), bf16[128,7936]{1,0:T(8,128)(2,1)}) %all-gather.12.cloned.1.call-update) | async-done | bytes 2031632 | tf_op jit(solution)/shard_map/all_gather | solution.py:58
  236.5 2.2 convolution_bitcast_fusion
  238.7 34.3 %psum.7 = f32[128,3]{0,1:T(4,128)S(1)} all-reduce(f32[128,3]{0,1:T(4,128)S(1)} %convolution_bitcast_fusion), channel_id=1, replica_groups=mesh['enc'=16,'vocab'=8,'grp'=2] {'vocab','grp'}, use_global_device_ids=true, to_apply=%region_3.4 | all-reduce | flops 384 | bytes 3072 | tf_op jit(solution)/shard_map/psum | solution.py:62
  273.0 15.7 %all-gather = f32[16,3,128]{2,1,0:T(4,128)S(1)} all-gather(f32[1,3,128]{2,1,0:T(4,128)S(1)} %bitcast.17), channel_id=1, replica_groups=mesh['enc'=16,'vocab'=8,'grp'=2] {'enc'}, dimensions={0}, use_global_device_ids=true | all-gather | bytes 26112 | tf_op jit(solution)/shard_map/all_gather | solution.py:63
  288.7 0.0 copy-done.1
  288.8 0.6 subtract_reduce_fusion
  289.4 0.0 copy-start
  289.4 2.7 fusion.14
  292.0 0.0 reduce-scatter.2.cloned.1.call-update
  292.7 0.0 copy-done
  292.7 1.0 fusion.20
  293.8 61.7 %reduce-scatter.2.cloned.1.call-done = f32[8,7936]{1,0:T(8,128)} async-done(((f32[128,7936]{1,0:T(8,128)}), f32[8,7936]{1,0:T(8,128)}) %reduce-scatter.2.cloned.1.call-update) | async-done | bytes 253968 | tf_op jit(solution)/shard_map/reduce_scatter | solution.py:67
  (5 shorter events, 0.1 us)
Async XLA Ops:
  7.2 54.9 %all-gather.6.cloned.1.call-start = ((), (), s32[]{:S(2)}) async-start(), calls=%async_computation.1 | async-start | bytes 1671168 | tf_op jit(solution)/shard_map/all_gather | solution.py:50
  7.9 95.5 %all-gather.8.cloned.1.call-start = ((), (), s32[]{:S(2)}) async-start(), calls=%async_computation.2 | async-start | bytes 2228224 | tf_op jit(solution)/shard_map/all_gather | solution.py:17
  8.6 187.9 %all-gather.10.cloned.1.call-start = ((), (), s32[]{:S(2)}) async-start(), calls=%async_computation.3 | async-start | bytes 17268736 | tf_op jit(solution)/shard_map/all_gather | solution.py:54
  9.4 227.2 %all-gather.12.cloned.1.call-start = ((), (), s32[]{:S(2)}) async-start(), calls=%async_computation.4 | async-start | bytes 2158592 | tf_op jit(solution)/shard_map/all_gather | solution.py:58
  10.0 345.5 %reduce-scatter.2.cloned.1.call-start = ((), (), s32[]{:S(2)}) async-start(), calls=%async_computation.5 | async-start | bytes 4317184 | tf_op jit(solution)/shard_map/reduce_scatter | solution.py:67
  114.0 82.6 %copy-start.2 = (f32[7936]{0:T(1024)S(1)}, f32[7936]{0:T(1024)}, u32[]{:S(2)}) copy-start(f32[7936]{0:T(1024)} %param.10) | copy-start | bytes 95236
  217.9 70.8 %copy-start.1 = (s32[128]{0:T(128)S(1)}, s32[128]{0:T(128)}, u32[]{:S(2)}) copy-start(s32[128]{0:T(128)} %param.13) | copy-start | bytes 1540
  289.4 3.3 copy-start
Sparse Core Ops, SparseCore 0:
  10.5 51.5 all-gather.5
  63.9 39.5 all-gather.7
  105.3 91.2 all-gather.9
  198.2 38.2 all-gather.11
  292.2 63.2 reduce-scatter.1
where the time goes:
time: 363 us
  waiting for transfers between devices  248 us (68%)
  blocking collectives  50 us (14%)
  matrix products  37.8 us (10%)
  between operations  15.6 us (4%)
  other arithmetic  12 us (3%)
    all_gather x1, waiting for transfers between devices, per_device(): lax.all_gather(head_weight, 'enc', axis=0, tiled=True)  82.1 us
    reduce_scatter x1, waiting for transfers between devices, per_device(): lax.psum_scatter(jnp.dot(own_grad, pass_reps, preferred_element_type=jnp....  61.7 us
    all_gather x1, waiting for transfers between devices, per_device(): features_all = lax.all_gather(hidden, ('vocab', 'grp'), axis=1, tiled=True)  50.6 us
    all_gather x1, waiting for transfers between devices, project(): lax.all_gather(dense_weight, 'enc', axis=0, tiled=True)  41.4 us
    psum x1, blocking collectives, per_device(): local_scores = lax.psum(partial_value, ('vocab', 'grp'))  34.3 us
    dot_general x1, matrix products, per_device(): jnp.dot(normed, lax.all_gather(head_weight, 'enc', axis=0, tiled=True), p...  21.4 us
    all_gather x1, blocking collectives, per_device(): scores = lax.all_gather(local_scores, 'enc', axis=1, tiled=True)  15.7 us
    dot_general x1, matrix products, project(): jnp.dot(in_rows, lax.all_gather(dense_weight, 'enc', axis=0, tiled=True),...  10.5 us
  transfers between devices with their start and end apart: 5, of which 5 were waited for; matrix products, arithmetic and copies ran while one was open for 12% of the time, Pallas kernels for 0%

commit v1 on v0

--- a/solution.py
+++ b/solution.py
@@ -2,6 +2,15 @@
 import jax.numpy as jnp
 from jax import lax
 from jax.sharding import PartitionSpec as P
+
+
+def _point_view(body, d0=0):
+    mesh_dim = "enc"
+    cores_n = lax.axis_size(mesh_dim)
+    pieces_in = tuple((cores_n if i0 == d0 else 1 for i0 in range(body.ndim)))
+    return lax.all_to_all(
+        jnp.tile(body, pieces_in), mesh_dim, split_axis=d0, concat_axis=d0, tiled=True
+    )
 
 
 def finish_norm(pre_act):
@@ -49,11 +58,7 @@
     enc_index = lax.axis_index("enc")
     features_all = lax.all_gather(hidden, ("vocab", "grp"), axis=1, tiled=True)
     normed = project(features_all, dense_weight)
-    logits = jnp.dot(
-        normed,
-        lax.all_gather(head_weight, "enc", axis=0, tiled=True),
-        preferred_element_type=jnp.float32,
-    )
+    logits = jnp.dot(normed, _point_view(head_weight), preferred_element_type=jnp.float32)
     pass_reps = pool_reps(logits + head_bias, lengths, seq_len)
     all_queries = lax.all_gather(queries, "enc", axis=0, tiled=True)
     partial_value = lax.dot_general(

time: 363 us -> 553 us (1.52)
  waiting for transfers between devices: 248 us -> 423 us
  starting transfers between devices: 0.19 us -> 8.9 us
  local copies, waits for them, and re-layouts: 0.03 us -> 6.68 us
    all_to_all x0 -> x1, waiting for transfers between devices: none -> 249 us  [_point_view(): lax.all_to_all(jnp.tile(body, pieces_in), mesh_dim, split_axis=d0, concat...]
    all_gather x1 -> x0, waiting for transfers between devices: 82.1 us -> none  [per_device(): lax.all_gather(head_weight, 'enc', axis=0, tiled=True)]
    all_gather x1, waiting for transfers between devices: 41.4 us -> 58.3 us  [project(): lax.all_gather(dense_weight, 'enc', axis=0, tiled=True)]
    all_gather x1, waiting for transfers between devices: 9.17 us -> 0.02 us  [per_device(): all_queries = lax.all_gather(queries, 'enc', axis=0, tiled=True)]
    all_to_all x0 -> x1, starting transfers between devices: none -> 8.75 us  [_point_view(): lax.all_to_all(jnp.tile(body, pieces_in), mesh_dim, split_axis=d0, concat...]
    another operation x0 -> x1, local copies, waits for them, and re-layouts: none -> 6.65 us  [_point_view(): jnp.tile(body, pieces_in)]
  transfers between devices with their start and end apart: 5 -> 5, of which waited for: 5 -> 4; matrix products, arithmetic and copies ran while one was open for 12% -> 8% of each run, Pallas kernels for 0% -> 0%
where the time goes in v1:
time: 553 us
  waiting for transfers between devices  423 us (76%)
  blocking collectives  50.5 us (9%)
  matrix products  37.7 us (7%)
  between operations  15.6 us (3%)
  other arithmetic  10.6 us (2%)
  starting transfers between devices  8.9 us (2%)
  local copies, waits for them, and re-layouts  6.68 us (1%)
    all_to_all x1, waiting for transfers between devices, _point_view(): lax.all_to_all(jnp.tile(body, pieces_in), mesh_dim, split_axis=d0, concat...  249 us
    reduce_scatter x1, waiting for transfers between devices, per_device(): lax.psum_scatter(jnp.dot(own_grad, pass_reps, preferred_element_type=jnp....  61.8 us
    all_gather x1, waiting for transfers between devices, project(): lax.all_gather(dense_weight, 'enc', axis=0, tiled=True)  58.3 us
    all_gather x1, waiting for transfers between devices, per_device(): features_all = lax.all_gather(hidden, ('vocab', 'grp'), axis=1, tiled=True)  51.1 us
    psum x1, blocking collectives, per_device(): local_scores = lax.psum(partial_value, ('vocab', 'grp'))  34.6 us
    dot_general x1, matrix products, per_device(): jnp.dot(normed, _point_view(head_weight), preferred_element_type=jnp.floa...  21.3 us
    all_gather x1, blocking collectives, per_device(): scores = lax.all_gather(local_scores, 'enc', axis=1, tiled=True)  15.9 us
  transfers between devices with their start and end apart: 5, of which 4 were waited for; matrix products, arithmetic and copies ran while one was open for 8% of the time, Pallas kernels for 0%

profile of v1, /device:TPU:2, one launch (start us, length us, event | category | flops | bytes accessed | tf_op | source)
XLA Modules:
  0.0 552.7 jit_solution(10954221380074742720)
XLA Ops:
  7.2 6.6 %tile.2 = bf16[16,64,7936]{2,1,0:T(8,128)(2,1)} broadcast(bf16[64,7936]{1,0:T(8,128)(2,1)} %param.9), dimensions={1,2} | broadcast | bytes 17268736 | tf_op jit(solution)/shard_map/tile | solution.py:12
  13.8 0.0 copy-start.3
  13.8 0.0 copy-start.1
  13.8 8.7 %all-to-all-start = ((bf16[16,64,7936]{2,1,0:T(8,128)(2,1)}), bf16[16,64,7936]{2,1,0:T(8,128)(2,1)}, u32[]{:S(2)}, u32[]{:S(2)}) async-start(bf16[16,64,7936]{2,1,0:T(8,128)(2,1)} %tile.2), calls=%async_computation | async-start | bytes 32505856 | tf_op jit(solution)/shard_map/all_to_all | solution.py:11
  22.6 0.0 all-gather.5.cloned.1.call-start
  22.6 0.7 all-gather.5.cloned.1.call-update
  23.3 0.0 all-gather.7.cloned.1.call-start
  23.4 0.7 all-gather.7.cloned.1.call-update
  24.1 0.0 all-gather.9.cloned.1.call-start
  24.1 0.7 all-gather.9.cloned.1.call-update
  24.8 0.0 reduce-scatter.2.cloned.1.call-start
  24.8 0.0 copy-done.3
  24.9 0.1 iota_compare_fusion.1
  24.9 0.0 copy-done.1
  24.9 51.1 %all-gather.5.cloned.1.call-done = bf16[768,1024]{0,1:T(8,128)(2,1)} async-done(((bf16[768,64]{0,1:T(8,128)(2,1)}), bf16[768,1024]{0,1:T(8,128)(2,1)}) %all-gather.5.cloned.1.call-update) | async-done | bytes 1572880 | tf_op jit(solution)/shard_map/all_gather | solution.py:59
  76.1 58.3 %all-gather.7.cloned.1.call-done = bf16[1024,1024]{1,0:T(8,128)(2,1)} async-done(((bf16[64,1024]{1,0:T(8,128)(2,1)}), bf16[1024,1024]{1,0:T(8,128)(2,1)}) %all-gather.7.cloned.1.call-update) | async-done | bytes 2097168 | tf_op jit(solution)/shard_map/all_gather | solution.py:26
  134.4 10.5 %fusion.17 = (f32[768]{0:T(1024)S(1)}, f32[768,1024]{1,0:T(8,128)S(1)}) fusion(bf16[768,1024]{0,1:T(8,128)(2,1)} %all-gather.5.cloned.1.call-done, bf16[1024,1024]{1,0:T(8,128)(2,1)} %all-gather.7.cloned.1.call-done), kind=kOutput, calls=%fused_computation.41 | convolution fusion | flops 1661730048 | bytes 6818816 | tf_op jit(solution)/shard_map/dot_general | solution.py:24
  145.0 0.0 copy-start.2
  145.0 0.4 multiply_reduce_fusion
  145.4 249.2 %all-to-all-done = bf16[16,64,7936]{2,1,0:T(8,128)(2,1)} async-done(((bf16[16,64,7936]{2,1,0:T(8,128)(2,1)}), bf16[16,64,7936]{2,1,0:T(8,128)(2,1)}, u32[]{:S(2)}, u32[]{:S(2)}) %all-to-all-start) | async-done | bytes 16252960 | tf_op jit(solution)/shard_map/all_to_all | solution.py:11
  394.7 0.0 copy-done.2
  394.7 21.3 %convolution_add_fusion = f32[768,7936]{1,0:T(8,128)} fusion(bf16[1024,7936]{1,0:T(8,128)(2,1)} %bitcast, f32[7936]{0:T(1024)S(1)} %copy-done.2, f32[768,1024]{1,0:T(8,128)S(1)} %get-tuple-element.8, f32[768]{0:T(1024)S(1)} %add_rsqrt_fusion, f32[768]{0:T(1024)S(1)} %broadcast_multiply_fusion), kind=kOutput, calls=%fused_computation.1 | convolution fusion | flops 12490702848 | bytes 43815936 | tf_op jit(solution)/shard_map/dot_general | solution.py:61
  416.0 9.4 %select_reduce_fusion = f32[3,7936]{1,0:T(4,128)S(1)} fusion(f32[3,256,7936]{2,1,0:T(8,128)} %bitcast.15, pred[3,256]{1,0:T(4,128)(4,1)S(1)} %iota_compare_fusion.1), kind=kLoop, calls=%fused_computation | loop fusion | flops 12165888 | bytes 24475392 | tf_op jit(solution)/shard_map/reduce_max | solution.py:38
  425.4 0.0 all-gather.9.cloned.1.call-done
  425.4 2.2 convolution_bitcast_fusion
  427.6 34.6 %psum.7 = f32[128,3]{0,1:T(4,128)S(1)} all-reduce(f32[128,3]{0,1:T(4,128)S(1)} %convolution_bitcast_fusion), channel_id=1, replica_groups=mesh['enc'=16,'vocab'=8,'grp'=2] {'vocab','grp'}, use_global_device_ids=true, to_apply=%region_3.4 | all-reduce | flops 384 | bytes 3072 | tf_op jit(solution)/shard_map/psum | solution.py:67
  462.2 15.9 %all-gather = f32[16,3,128]{2,1,0:T(4,128)S(1)} all-gather(f32[1,3,128]{2,1,0:T(4,128)S(1)} %bitcast.18), channel_id=1, replica_groups=mesh['enc'=16,'vocab'=8,'grp'=2] {'enc'}, dimensions={0}, use_global_device_ids=true | all-gather | bytes 26112 | tf_op jit(solution)/shard_map/all_gather | solution.py:68
  478.2 0.6 subtract_reduce_fusion
  478.8 0.0 copy-start
  478.8 2.7 fusion.14
  481.5 0.0 reduce-scatter.2.cloned.1.call-update
  482.1 0.0 copy-done
  482.2 1.0 fusion.20
  483.2 61.8 %reduce-scatter.2.cloned.1.call-done = f32[8,7936]{1,0:T(8,128)} async-done(((f32[128,7936]{1,0:T(8,128)}), f32[8,7936]{1,0:T(8,128)}) %reduce-scatter.2.cloned.1.call-update) | async-done | bytes 253968 | tf_op jit(solution)/shard_map/reduce_scatter | solution.py:72
  (6 shorter events, 0.1 us)
Async XLA Ops:
  13.8 11.0 %copy-start.3 = (s32[3]{0:T(128)S(1)}, s32[3]{0:T(128)}, u32[]{:S(2)}) copy-start(s32[3]{0:T(128)} %param.11) | copy-start | bytes 40
  13.8 11.1 %copy-start.1 = (s32[128]{0:T(128)S(1)}, s32[128]{0:T(128)}, u32[]{:S(2)}) copy-start(s32[128]{0:T(128)} %param.13) | copy-start | bytes 1540
  13.8 380.9 %all-to-all-start = ((bf16[16,64,7936]{2,1,0:T(8,128)(2,1)}), bf16[16,64,7936]{2,1,0:T(8,128)(2,1)}, u32[]{:S(2)}, u32[]{:S(2)}) async-start(bf16[16,64,7936]{2,1,0:T(8,128)(2,1)} %tile.2), calls=%async_computation | async-start | bytes 32505856 | tf_op jit(solution)/shard_map/all_to_all | solution.py:11
  22.6 53.5 %all-gather.5.cloned.1.call-start = ((), (), s32[]{:S(2)}) async-start(), calls=%async_computation.2 | async-start | bytes 1671168 | tf_op jit(solution)/shard_map/all_gather | solution.py:59
  23.3 111.1 %all-gather.7.cloned.1.call-start = ((), (), s32[]{:S(2)}) async-start(), calls=%async_computation.3 | async-start | bytes 2228224 | tf_op jit(solution)/shard_map/all_gather | solution.py:26
  24.1 401.4 %all-gather.9.cloned.1.call-start = ((), (), s32[]{:S(2)}) async-start(), calls=%async_computation.4 | async-start | bytes 2158592 | tf_op jit(solution)/shard_map/all_gather | solution.py:63
  24.8 520.2 %reduce-scatter.2.cloned.1.call-start = ((), (), s32[]{:S(2)}) async-start(), calls=%async_computation.5 | async-start | bytes 4317184 | tf_op jit(solution)/shard_map/reduce_scatter | solution.py:72
  145.0 249.7 %copy-start.2 = (f32[7936]{0:T(1024)S(1)}, f32[7936]{0:T(1024)}, u32[]{:S(2)}) copy-start(f32[7936]{0:T(1024)} %param.10) | copy-start | bytes 95236
  478.8 3.3 copy-start
Sparse Core Ops, SparseCore 0:
  25.9 50.1 all-gather.4
  77.9 56.4 all-gather.6
  136.3 79.5 all-gather.8
  481.6 63.3 reduce-scatter.1
